TPU v7x, 32 devices: a whole 2x2x4 slice. The times are simulated.
32 devices in a mesh: groups: 2 (over x), tm: 16 (over z, y, core).
Axes of the slice: x: 2, y: 2, z: 4, core: 2. Of those that a mesh axis runs over, the one named last changes fastest.
Arguments:
- states: bfloat16 [4096, 2, 1024], P('tm', 'groups'), parts along dimension 1, may hold values from -6 to 6
- goals: bfloat16 [4096, 2, 1024], P('tm', 'groups'), parts along dimension 1, may hold values from -6 to 6
- pos_offset: int32 [16, 2, 8], P('tm', 'groups'), parts along dimension 1, may hold values from 0 to 15
- neg_blocks: int32 [16, 2, 16], P('tm', 'groups'), parts along dimension 1, may hold values from 0 to 15
Outputs:
- loss_mean: float32 [2], P('groups'), parts along dimension 0
- grad_states: float32 [4096, 2, 1024], P('tm', 'groups'), parts along dimension 1
- grad_goals: float32 [4096, 2, 1024], P('tm', 'groups'), parts along dimension 1
There are 2 independent parts, one for each index of `groups`. A program takes and returns all parts, laid end to end along the dimension named above; each array names one. Nothing has to cross between parts.
All inputs are finite; a program needn't handle non-finite values.
Results may differ from a plain program's by a relative error of at most 0.012.
Values may be sent and summed in bfloat16 or wider, within the bound.
No kernel may reach another device: no remote copies, remote signals or barrier semaphores. Data moves between devices by JAX's collectives and lax.ppermute only.
A program may use at most 128 MiB of HBM per device.

v0:
```python
import math
import jax
import jax.numpy as jnp
from jax import lax
from jax.sharding import PartitionSpec as P

E = 1024
L = 256


def pair_weights(pos_offset, neg_blocks, row_first, row_count, col_count):
    block_count = row_count // L
    row_blocks = row_first // L + jnp.arange(block_count, dtype=jnp.int32)
    col_times = jnp.arange(col_count, dtype=jnp.int32)
    col_blocks = col_times // L
    targets = row_blocks[:, None, None] + pos_offset
    pos_count = jnp.sum((targets[..., None] == col_blocks).astype(jnp.float32), axis=2)
    neg_count = jnp.sum((neg_blocks[..., None] == col_blocks).astype(jnp.float32), axis=2)
    pos_count = jnp.repeat(jnp.swapaxes(pos_count, 0, 1), L, axis=1)
    neg_count = jnp.repeat(jnp.swapaxes(neg_count, 0, 1), L, axis=1)
    row_times = row_first + jnp.arange(row_count, dtype=jnp.int32)
    later_mask = (col_times[None, :] > row_times[:, None]).astype(jnp.float32)
    return (pos_count * later_mask, neg_count)


def score_terms(anchor_rows, goal_rows, pos_weight, neg_weight):
    inv_root = 1.0 / math.sqrt(E)
    scores = (
        jnp.einsum("qte,kte->tqk", anchor_rows, goal_rows, preferred_element_type=jnp.float32)
        * inv_root
    )
    loss_sum = jnp.sum(pos_weight * jax.nn.softplus(-scores) + neg_weight * jax.nn.softplus(scores))
    slopes = neg_weight * jax.nn.sigmoid(scores) - pos_weight * jax.nn.sigmoid(-scores)
    return (loss_sum, (slopes * inv_root).astype(jnp.bfloat16))


def per_device(states, goals, pos_offset, neg_blocks):
    row_count = states.shape[0]
    traj_count = states.shape[1]
    steps_all = row_count * lax.axis_size("tm")
    row_first = lax.axis_index("tm") * row_count
    goal_piece = lax.all_gather(goals, "tm", axis=0, tiled=True)
    col_count = goal_piece.shape[0]
    pos_weight, neg_weight = pair_weights(pos_offset, neg_blocks, row_first, row_count, col_count)
    loss_sum, coeffs = score_terms(states, goal_piece, pos_weight, neg_weight)
    grad_rows = jnp.einsum("tqk,kte->qte", coeffs, goal_piece, preferred_element_type=jnp.float32)
    loss_sum, coeffs, grad_rows = (loss_sum, coeffs, grad_rows)
    folded = (grad_rows, loss_sum, coeffs)
    grad_states = folded[0]
    loss_sum = folded[1]
    coeff_all = folded[2]
    grad_goals = lax.psum_scatter(
        jnp.einsum("tqk,qte->kte", coeff_all, states, preferred_element_type=jnp.float32).astype(
            jnp.bfloat16
        ),
        "tm",
        scatter_dimension=0,
        tiled=True,
    ).astype(jnp.float32)
    loss_all = lax.psum(loss_sum, "tm")
    loss_mean = (loss_all / (traj_count * steps_all)).reshape(1)
    return (loss_mean, grad_states, grad_goals)


def solution(mesh):
    in_specs = (
        P("tm", "groups", None),
        P("tm", "groups", None),
        P("tm", "groups", None),
        P("tm", "groups", None),
    )
    out_specs = (P("groups"), P("tm", "groups", None), P("tm", "groups", None))
    return jax.shard_map(
        per_device, mesh=mesh, in_specs=in_specs, out_specs=out_specs, check_vma=False
    )
```

profile of v0, /device:TPU:0, one launch (start us, length us, event | category | flops | bytes accessed | tf_op | source)
XLA Modules:
  0.0 219.8 jit_solution(17836653208547374864)
XLA Ops:
  7.2 0.0 copy-start
  7.2 0.0 all-gather.2.cloned.1.call-start
  7.2 0.7 all-gather.2.cloned.1.call-update
  7.9 0.0 reduce-scatter.2.cloned.1.call-start
  8.0 0.7 add_bitcast_fusion
  8.7 0.1 convert_reduce_fusion.1
  8.8 0.8 convert_reduce_fusion
  9.6 77.6 %all-gather.2.cloned.1.call-done = bf16[4096,1,1024]{2,0,1:T(8,128)(2,1)} async-done(((bf16[256,1,1024]{2,0,1:T(8,128)(2,1)}), bf16[4096,1,1024]{2,0,1:T(8,128)(2,1)}) %all-gather.2.cloned.1.call-update) | async-done | bytes 8388624 | tf_op jit(solution)/shard_map/all_gather | solution.py:42
  87.2 0.0 copy-done
  87.2 11.5 %fusion.8 = (f32[]{:T(128)}, f32[256,4096]{1,0:T(8,128)S(1)}) fusion(f32[4096]{0:T(1024)S(1)} %convert_reduce_fusion, f32[4096]{0:T(1024)S(1)} %convert_reduce_fusion.1, s32[256]{0:T(256)S(1)} %iota_add_fusion, bf16[4096,1,1024]{2,0,1:T(8,128)(2,1)} %all-gather.2.cloned.1.call-done, bf16[256,1,1024]{2,0,1:T(8,128)(2,1)S(1)} %copy-done), kind=kOutput, calls=%fused_computation.11 | convolution fusion | flops 2168455168 | bytes 13140996 | tf_op jit(solution)/shard_map/qte,kte->tqk/dot_general | solution.py:29
  98.7 0.0 copy-start.1
  98.7 1.9 copy-done.1
  100.6 6.2 %convert_bitcast_fusion = bf16[4096,1,1024]{2,0,1:T(8,128)(2,1)} fusion(bf16[256,1,1024]{2,0,1:T(8,128)(2,1)S(1)} %copy-done, f32[256,4096]{1,0:T(8,128)S(1)} %get-tuple-element.10, f32[4096]{0:T(1024)S(1)} %convert_reduce_fusion, f32[4096]{0:T(1024)S(1)} %convert_reduce_fusion.1, s32[256]{0:T(256)S(1)} %iota_add_fusion), kind=kOutput, calls=%fused_computation.6 | convolution fusion | flops 2164260864 | bytes 13140992 | tf_op jit(solution)/shard_map/tqk,qte->kte/dot_general | solution.py:53
  106.8 0.0 reduce-scatter.2.cloned.1.call-update
  106.8 32.1 %psum.7 = f32[]{:T(128)} all-reduce(f32[]{:T(128)} %get-tuple-element.9), channel_id=1, replica_groups=mesh['groups'=2,'tm'=16] {'tm'}, use_global_device_ids=true, to_apply=%region_3.4 | all-reduce | flops 1 | bytes 8 | tf_op jit(solution)/shard_map/psum | solution.py:60
  138.9 8.2 %fusion.13 = f32[256,1,1024]{2,0,1:T(8,128)S(1)} fusion(bf16[4096,1,1024]{2,0,1:T(8,128)(2,1)} %all-gather.2.cloned.1.call-done, f32[256,4096]{1,0:T(8,128)} %copy-done.1, f32[4096]{0:T(1024)S(1)} %convert_reduce_fusion, f32[4096]{0:T(1024)S(1)} %convert_reduce_fusion.1, s32[256]{0:T(256)S(1)} %iota_add_fusion), kind=kOutput, calls=%fused_computation.18 | convolution fusion | flops 2160066560 | bytes 13665280 | tf_op jit(solution)/shard_map/tqk,kte->qte/dot_general | solution.py:46
  147.1 2.0 copy.9
  149.8 59.2 %reduce-scatter.2.cloned.1.call-done = bf16[256,1,1024]{2,0,1:T(8,128)(2,1)} async-done(((bf16[4096,1,1024]{2,0,1:T(8,128)(2,1)}), bf16[256,1,1024]{2,0,1:T(8,128)(2,1)}) %reduce-scatter.2.cloned.1.call-update) | async-done | bytes 524304 | tf_op jit(solution)/shard_map/reduce_scatter | solution.py:52
  209.0 2.8 %copy.10 = f32[256,1,1024]{2,1,0:T(1,128)} copy(bf16[256,1,1024]{2,0,1:T(8,128)(2,1)} %reduce-scatter.2.cloned.1.call-done) | data formatting | bytes 1572864
  (2 shorter events, 0.0 us)
Async XLA Ops:
  7.2 80.0 %copy-start = (bf16[256,1,1024]{2,0,1:T(8,128)(2,1)S(1)}, bf16[256,1,1024]{2,0,1:T(8,128)(2,1)}, u32[]{:S(2)}) copy-start(bf16[256,1,1024]{2,0,1:T(8,128)(2,1)} %param.4) | copy-start | bytes 1572868
  7.2 80.0 %all-gather.2.cloned.1.call-start = ((), (), s32[]{:S(2)}) async-start(), calls=%async_computation.1 | async-start | bytes 8912896 | tf_op jit(solution)/shard_map/all_gather | solution.py:42
  7.9 201.1 %reduce-scatter.2.cloned.1.call-start = ((), (), s32[]{:S(2)}) async-start(), calls=%async_computation.2 | async-start | bytes 8912896 | tf_op jit(solution)/shard_map/reduce_scatter | solution.py:52
  98.7 1.9 copy-start.1
Sparse Core Ops, SparseCore 0:
  10.2 77.0 all-gather.1
  107.0 102.0 reduce-scatter.1
where the time goes:
time: 220 us
  waiting for transfers between devices  138 us (63%)
  blocking collectives  32.1 us (15%)
  matrix products  25.9 us (12%)
  between operations  15.9 us (7%)
  local copies, waits for them, and re-layouts  6.8 us (3%)
    all_gather x1, waiting for transfers between devices, per_device(): goal_piece = lax.all_gather(goals, 'tm', axis=0, tiled=True)  77.6 us
    reduce_scatter x1, waiting for transfers between devices, per_device(): lax.psum_scatter(jnp.einsum('tqk,qte->kte', coeff_all, states, preferred_...  59.2 us
    psum x1, blocking collectives, per_device(): loss_all = lax.psum(loss_sum, 'tm')  32.1 us
    dot_general x1, matrix products, score_terms(): jnp.einsum('qte,kte->tqk', anchor_rows, goal_rows, preferred_element_type...  11.5 us
    dot_general x1, matrix products, per_device(): jnp.einsum('tqk,kte->qte', coeffs, goal_piece, preferred_element_type=jnp...  8.22 us
    unnamed x6, local copies, waits for them, and re-layouts  6.8 us
    dot_general x1, matrix products, per_device(): jnp.einsum('tqk,qte->kte', coeff_all, states, preferred_element_type=jnp....  6.2 us
  transfers between devices with their start and end apart: 2, of which 2 were waited for; matrix products, arithmetic and copies ran while one was open for 5% of the time, Pallas kernels for 0%

commit v1 on v0

--- a/solution.py
+++ b/solution.py
@@ -39,7 +39,11 @@
     traj_count = states.shape[1]
     steps_all = row_count * lax.axis_size("tm")
     row_first = lax.axis_index("tm") * row_count
-    goal_piece = lax.all_gather(goals, "tm", axis=0, tiled=True)
+    length = lax.axis_size("tm")
+    repeats = [length if d == 0 else 1 for d in range(goals.ndim)]
+    goal_piece = lax.all_to_all(
+        jnp.tile(goals, repeats), "tm", split_axis=0, concat_axis=0, tiled=True
+    )
     col_count = goal_piece.shape[0]
     pos_weight, neg_weight = pair_weights(pos_offset, neg_blocks, row_first, row_count, col_count)
     loss_sum, coeffs = score_terms(states, goal_piece, pos_weight, neg_weight)

time: 220 us -> 387 us (1.76)
  waiting for transfers between devices: 138 us -> 206 us
  local copies, waits for them, and re-layouts: 6.8 us -> 43.7 us
  blocking collectives: 32.1 us -> 65.5 us
  other arithmetic: 1.56 us -> 12.9 us
  matrix products: 25.9 us -> 34 us
  starting transfers between devices: 0.08 us -> 7.82 us
    all_to_all x0 -> x1, waiting for transfers between devices: none -> 150 us  [per_device(): lax.all_to_all(jnp.tile(goals, repeats), 'tm', split_axis=0, concat_axis=...]
    all_gather x1 -> x0, waiting for transfers between devices: 77.6 us -> none  [per_device(): goal_piece = lax.all_gather(goals, 'tm', axis=0, tiled=True)]
    psum x1, blocking collectives: 32.1 us -> 65.5 us  [per_device(): loss_all = lax.psum(loss_sum, 'tm')]
    unnamed x6 -> x14, local copies, waits for them, and re-layouts: 6.8 us -> 37.8 us
    another operation x0 -> x1, other arithmetic: none -> 12.7 us  [per_device(): jnp.tile(goals, repeats)]
    all_to_all x0 -> x1, starting transfers between devices: none -> 7.6 us  [per_device(): lax.all_to_all(jnp.tile(goals, repeats), 'tm', split_axis=0, concat_axis=...]
    another operation x0 -> x2, local copies, waits for them, and re-layouts: none -> 5.9 us  [per_device(): jnp.tile(goals, repeats)]
    dot_general x1, matrix products: 11.5 us -> 16.4 us  [score_terms(): jnp.einsum('qte,kte->tqk', anchor_rows, goal_rows, preferred_element_type...]
  transfers between devices with their start and end apart: 2 -> 2, of which waited for: 2 -> 2; matrix products, arithmetic and copies ran while one was open for 5% -> 4% of each run, Pallas kernels for 0% -> 0%
where the time goes in v1:
time: 387 us; the launch traced here: 386 us
  waiting for transfers between devices  206 us (53%)
  blocking collectives  65.5 us (17%)
  local copies, waits for them, and re-layouts  43.7 us (11%)
  matrix products  34 us (9%)
  between operations  15.9 us (4%)
  other arithmetic  12.9 us (3%)
  starting transfers between devices  7.82 us (2%)
    all_to_all x1, waiting for transfers between devices, per_device(): lax.all_to_all(jnp.tile(goals, repeats), 'tm', split_axis=0, concat_axis=...  150 us
    psum x1, blocking collectives, per_device(): loss_all = lax.psum(loss_sum, 'tm')  65.5 us
    reduce_scatter x1, waiting for transfers between devices, per_device(): lax.psum_scatter(jnp.einsum('tqk,qte->kte', coeff_all, states, preferred_...  55.9 us
    unnamed x14, local copies, waits for them, and re-layouts  37.8 us
    dot_general x1, matrix products, score_terms(): jnp.einsum('qte,kte->tqk', anchor_rows, goal_rows, preferred_element_type...  16.4 us
    another operation x1, other arithmetic, per_device(): jnp.tile(goals, repeats)  12.7 us
    dot_general x1, matrix products, per_device(): jnp.einsum('tqk,kte->qte', coeffs, goal_piece, preferred_element_type=jnp...  11.4 us
  transfers between devices with their start and end apart: 2, of which 2 were waited for; matrix products, arithmetic and copies ran while one was open for 4% of the time, Pallas kernels for 0%

profile of v1, /device:TPU:0, one launch (start us, length us, event | category | flops | bytes accessed | tf_op | source)
XLA Modules:
  0.0 385.7 jit_solution(15526041602857871771)
XLA Ops:
  7.2 0.0 copy-start
  7.2 5.4 %tile.12 = bf16[16,256,1024]{2,1,0:T(8,128)(2,1)} broadcast(bf16[256,1024]{1,0:T(8,128)(2,1)} %bitcast.37), dimensions={1,2} | broadcast | bytes 8912896 | tf_op jit(solution)/shard_map/tile | solution.py:45
  12.6 0.5 broadcast.169
  13.1 12.7 %reduce.4 = bf16[4096,1024]{1,0:T(8,128)(2,1)} reduce(bf16[4096,1,1024]{2,0,1:T(8,128)(2,1)} %bitcast.36, bf16[]{:T(256)} %broadcast.169), dimensions={1}, to_apply=%copy.14.reduce_sub_computation | reduce | bytes 16777218 | tf_op jit(solution)/shard_map/tile | solution.py:45
  25.8 14.5 %reshape.226 = bf16[16,2,131072]{2,1,0:T(2,128)(2,1)} reshape(bf16[4096,1024]{1,0:T(8,128)(2,1)} %reduce.4) | data formatting | bytes 16777216
  40.3 0.0 copy-start.3
  40.3 0.0 copy-start.2
  40.3 7.6 %all-to-all-start = ((bf16[16,2,131072]{2,1,0:T(2,128)(2,1)}), bf16[16,2,131072]{2,1,0:T(2,128)(2,1)}, u32[]{:S(2)}, u32[]{:S(2)}) async-start(bf16[16,2,131072]{2,1,0:T(2,128)(2,1)} %reshape.226), calls=%async_computation | async-start | bytes 16777216 | tf_op jit(solution)/shard_map/all_to_all | solution.py:44
  47.9 0.2 reduce-scatter.2.cloned.1.call-start
  48.2 0.0 copy-done.3
  48.2 0.1 convert_reduce_fusion.1
  48.3 0.0 copy-done.2
  48.3 0.1 convert_reduce_fusion
  48.4 150.0 %all-to-all-done = bf16[16,2,131072]{2,1,0:T(2,128)(2,1)} async-done(((bf16[16,2,131072]{2,1,0:T(2,128)(2,1)}), bf16[16,2,131072]{2,1,0:T(2,128)(2,1)}, u32[]{:S(2)}, u32[]{:S(2)}) %all-to-all-start) | async-done | bytes 8388640 | tf_op jit(solution)/shard_map/all_to_all | solution.py:44
  198.5 16.4 %reshape.227 = bf16[4096,1,1024]{2,1,0:T(2,128)(2,1)} reshape(bf16[16,2,131072]{2,1,0:T(2,128)(2,1)} %all-to-all-done) | data formatting | bytes 16777216
  214.8 0.0 copy-done
  214.8 16.4 %fusion.8 = (f32[]{:T(128)}, f32[256,4096]{1,0:T(8,128)S(1)}) fusion(f32[4096]{0:T(1024)S(1)} %convert_reduce_fusion, f32[4096]{0:T(1024)S(1)} %convert_reduce_fusion.1, s32[256]{0:T(256)S(1)} %iota_add_fusion, bf16[4096,1,1024]{2,1,0:T(2,128)(2,1)} %reshape.227, bf16[256,1,1024]{2,0,1:T(8,128)(2,1)S(1)} %copy-done), kind=kOutput, calls=%fused_computation.11 | convolution fusion | flops 2168455168 | bytes 13140996 | tf_op jit(solution)/shard_map/qte,kte->tqk/dot_general | solution.py:29
  231.2 0.0 copy-start.4
  231.2 2.0 copy-done.4
  233.2 6.2 %convert_bitcast_fusion = bf16[4096,1,1024]{2,0,1:T(8,128)(2,1)} fusion(bf16[256,1,1024]{2,0,1:T(8,128)(2,1)S(1)} %copy-done, f32[256,4096]{1,0:T(8,128)S(1)} %get-tuple-element.16, f32[4096]{0:T(1024)S(1)} %convert_reduce_fusion, f32[4096]{0:T(1024)S(1)} %convert_reduce_fusion.1, s32[256]{0:T(256)S(1)} %iota_add_fusion), kind=kOutput, calls=%fused_computation.6 | convolution fusion | flops 2164260864 | bytes 13140992 | tf_op jit(solution)/shard_map/tqk,qte->kte/dot_general | solution.py:57
  239.4 0.0 reduce-scatter.2.cloned.1.call-update
  239.4 65.5 %psum.7 = f32[]{:T(128)} all-reduce(f32[]{:T(128)} %get-tuple-element.15), channel_id=1, replica_groups=mesh['groups'=2,'tm'=16] {'tm'}, use_global_device_ids=true, to_apply=%region_3.4 | all-reduce | flops 1 | bytes 8 | tf_op jit(solution)/shard_map/psum | solution.py:64
  304.9 0.0 copy-start.1
  304.9 11.4 %fusion.15 = f32[256,1,1024]{2,0,1:T(8,128)S(1)} fusion(bf16[4096,1,1024]{2,1,0:T(2,128)(2,1)} %reshape.227, f32[256,4096]{1,0:T(8,128)} %copy-done.4, f32[4096]{0:T(1024)S(1)} %convert_reduce_fusion, f32[4096]{0:T(1024)S(1)} %convert_reduce_fusion.1, s32[256]{0:T(256)S(1)} %iota_add_fusion), kind=kOutput, calls=%fused_computation.20 | convolution fusion | flops 2160066560 | bytes 13665280 | tf_op jit(solution)/shard_map/tqk,kte->qte/dot_general | solution.py:50
  316.3 2.0 copy.15
  319.0 55.9 %reduce-scatter.2.cloned.1.call-done = bf16[256,1,1024]{2,0,1:T(8,128)(2,1)} async-done(((bf16[4096,1,1024]{2,0,1:T(8,128)(2,1)}), bf16[256,1,1024]{2,0,1:T(8,128)(2,1)}) %reduce-scatter.2.cloned.1.call-update) | async-done | bytes 524304 | tf_op jit(solution)/shard_map/reduce_scatter | solution.py:56
  374.9 2.8 copy.16
  377.7 0.0 copy-done.1
  (3 shorter events, 0.0 us)
Async XLA Ops:
  7.2 207.7 %copy-start = (bf16[256,1,1024]{2,0,1:T(8,128)(2,1)S(1)}, bf16[256,1,1024]{2,0,1:T(8,128)(2,1)}, u32[]{:S(2)}) copy-start(bf16[256,1,1024]{2,0,1:T(8,128)(2,1)} %param.4) | copy-start | bytes 1572868
  40.3 7.9 %copy-start.3 = (s32[1,1,8]{2,1,0:T(1,128)S(1)}, s32[1,1,8]{2,1,0:T(1,128)}, u32[]{:S(2)}) copy-start(s32[1,1,8]{2,1,0:T(1,128)} %param.6) | copy-start | bytes 100
  40.3 8.0 %copy-start.2 = (s32[1,1,16]{2,1,0:T(1,128)S(1)}, s32[1,1,16]{2,1,0:T(1,128)}, u32[]{:S(2)}) copy-start(s32[1,1,16]{2,1,0:T(1,128)} %param.7) | copy-start | bytes 196
  40.3 158.2 %all-to-all-start = ((bf16[16,2,131072]{2,1,0:T(2,128)(2,1)}), bf16[16,2,131072]{2,1,0:T(2,128)(2,1)}, u32[]{:S(2)}, u32[]{:S(2)}) async-start(bf16[16,2,131072]{2,1,0:T(2,128)(2,1)} %reshape.226), calls=%async_computation | async-start | bytes 16777216 | tf_op jit(solution)/shard_map/all_to_all | solution.py:44
  47.9 327.0 %reduce-scatter.2.cloned.1.call-start = ((), (), s32[]{:S(2)}) async-start(), calls=%async_computation.2 | async-start | bytes 8912896 | tf_op jit(solution)/shard_map/reduce_scatter | solution.py:56
  231.2 2.0 copy-start.4
  304.9 72.8 %copy-start.1 = (bf16[256,1,1024]{2,0,1:T(8,128)(2,1)S(1)}, bf16[256,1,1024]{2,0,1:T(8,128)(2,1)}, u32[]{:S(2)}) copy-start(bf16[256,1,1024]{2,0,1:T(8,128)(2,1)} %param.4) | copy-start | bytes 1572868
Sparse Core Ops, SparseCore 0:
  239.5 135.2 reduce-scatter.1
